TPU v7x, 32 devices: a whole 2x2x4 slice. The times are simulated.
32 devices in a mesh: space: 8 (over z, x), field: 4 (over y, core).
Axes of the slice: x: 2, y: 2, z: 4, core: 2. Of those that a mesh axis runs over, the one named last changes fastest.
Arguments:
- composition_vector: float32 [4, 32, 32, 16, 128], P('field', None, 'space'), may hold values from -6 to 6
- filtered_motion: float32 [3, 32, 16, 128], P(None, 'space', 'field'), may hold values from -1.8 to 1.8
- spreading_strength: float32 [32, 16, 128], P('space', 'field'), may hold values from 0.02 to 0.12
- blend_relax_multiplier: float32 [32, 16, 128], P('space', 'field'), may hold values from 0.2 to 0.9
- thermal_level: float32 [32, 16, 128], P('space', 'field'), may hold values from 0.5 to 2
- brownian_jumps: float32 [2, 4, 3], P(None, 'field'), may hold values from -2.5 to 2.5
- left_bilinear_weights: bfloat16 [206, 32], replicated, may hold values from -1 to 1
- right_bilinear_weights: bfloat16 [206, 32], replicated, may hold values from -1 to 1
- species_yield_weights: bfloat16 [32, 206], replicated, may hold values from -0.4375 to 0.4375
- arrhenius_prefactor: float32 [206], replicated, may hold values from 0.3 to 3
- ignition_energy_ratio: float32 [206], replicated, may hold values from 0.2 to 2
Outputs:
- result: float32 [4, 32, 32, 16, 128], P('field', None, 'space')
All inputs are finite; a program needn't handle non-finite values.
Results may differ from a plain program's by a relative error of at most 0.00068.
Values sent between devices are 32-bit elements; how exact they have to be, the bound alone decides.
A program may use at most 64 MiB of HBM per device.

v0:
```python
import jax
import jax.numpy as jnp
from jax import lax
from jax.sharding import PartitionSpec as P

STEPS = 2
SUB = 5
chem_step = 0.2


def extended(value, sides, width):
    for axis, dim in sides:
        count, length = (lax.axis_size(axis), value.shape[dim])
        up = [(i, (i + 1) % count) for i in range(count)]
        down = [(j, i) for i, j in up]
        last = lax.slice_in_dim(value, length - width, length, axis=dim)
        leading = lax.slice_in_dim(value, 0, width, axis=dim)
        before = lax.ppermute(last, axis, up)
        after = lax.ppermute(leading, axis, down)
        value = jnp.concatenate([before, value, after], axis=dim)
    return value


def transport(padded, current, mean, filtered_motion, spreading_strength, mixing, wiener):
    x_plus = padded[:, 2:]
    x_minus = padded[:, :-2]
    y_plus = jnp.roll(current, -1, 2)
    y_minus = jnp.roll(current, 1, 2)
    z_plus = jnp.roll(current, -1, 3)
    z_minus = jnp.roll(current, 1, 3)
    grad_x = 0.5 * (x_plus - x_minus)
    grad_y = 0.5 * (y_plus - y_minus)
    grad_z = 0.5 * (z_plus - z_minus)
    laplace = x_plus + x_minus + y_plus + y_minus + z_plus + z_minus - 6.0 * current
    advect = filtered_motion[0] * grad_x + filtered_motion[1] * grad_y + filtered_motion[2] * grad_z
    noise = jnp.sqrt(2.0 * spreading_strength) * (
        wiener[0] * grad_x + wiener[1] * grad_y + wiener[2] * grad_z
    )
    return current - advect + spreading_strength * laplace + noise - mixing * (current - mean)


def react(block, arrhenius, left_bilinear_weights, right_bilinear_weights, species_yield_weights):
    for substep in range(SUB):
        lowered = block.astype(jnp.bfloat16)
        forward = jnp.dot(left_bilinear_weights, lowered, preferred_element_type=jnp.float32)
        backward = jnp.dot(right_bilinear_weights, lowered, preferred_element_type=jnp.float32)
        saturation = 1.0 + forward * forward + backward * backward
        rates = (arrhenius * forward * backward / saturation).astype(jnp.bfloat16)
        block = block + chem_step * jnp.dot(
            species_yield_weights, rates, preferred_element_type=jnp.float32
        )
    return block


def kinetic_yield_term(
    carried_ensemble,
    thermal_level,
    arrhenius_prefactor,
    ignition_energy_ratio,
    left_bilinear_weights,
    right_bilinear_weights,
    species_yield_weights,
):
    species_count, planes, vertical_extent, streamwise_extent = carried_ensemble.shape

    def one_plane(plane_index, current):
        starting_ensemble = jnp.asarray(plane_index).astype(jnp.int32)
        block = lax.dynamic_slice_in_dim(current, starting_ensemble, 1, 1).reshape(
            species_count, vertical_extent * streamwise_extent
        )
        enthalpy_output = lax.dynamic_slice_in_dim(thermal_level, starting_ensemble, 1, 0).reshape(
            1, vertical_extent * streamwise_extent
        )
        arrhenius = arrhenius_prefactor[:, None] * jnp.exp(
            -ignition_energy_ratio[:, None] / enthalpy_output
        )
        reacted = react(
            block, arrhenius, left_bilinear_weights, right_bilinear_weights, species_yield_weights
        )
        reacted = reacted.reshape(species_count, 1, vertical_extent, streamwise_extent)
        return lax.dynamic_update_slice_in_dim(current, reacted, starting_ensemble, 1)

    return lax.fori_loop(0, planes, one_plane, carried_ensemble)


def body(
    composition_vector,
    filtered_motion,
    spreading_strength,
    blend_relax_multiplier,
    thermal_level,
    brownian_jumps,
    left_bilinear_weights,
    right_bilinear_weights,
    species_yield_weights,
    arrhenius_prefactor,
    ignition_energy_ratio,
):
    fields = lax.axis_size("field")
    motion_lookup, spreading_gradient_sum, subgrid_blend_sum, thermal_lookup = (
        lax.all_gather(filtered_motion, "field", axis=2, tiled=True),
        lax.all_gather(spreading_strength, "field", axis=1, tiled=True),
        lax.all_gather(blend_relax_multiplier, "field", axis=1, tiled=True),
        lax.all_gather(thermal_level, "field", axis=1, tiled=True),
    )
    current = composition_vector[0]
    for step in range(STEPS):
        mean = lax.psum(current, "field") / fields
        padded = extended(current, (("space", 1),), 1)
        carried_ensemble = transport(
            padded,
            current,
            mean,
            motion_lookup,
            spreading_gradient_sum,
            subgrid_blend_sum,
            brownian_jumps[step, 0],
        )
        current = kinetic_yield_term(
            carried_ensemble,
            thermal_lookup,
            arrhenius_prefactor,
            ignition_energy_ratio,
            left_bilinear_weights,
            right_bilinear_weights,
            species_yield_weights,
        )
    return current[None]


def solution(mesh):
    return jax.shard_map(
        body,
        mesh=mesh,
        in_specs=(
            P("field", None, "space", None, None),
            P(None, "space", "field", None),
            P("space", "field", None),
            P("space", "field", None),
            P("space", "field", None),
            P(None, "field", None),
            P(),
            P(),
            P(),
            P(),
            P(),
        ),
        out_specs=P("field", None, "space", None, None),
        check_vma=False,
    )
```

profile of v0, /device:TPU:0, one launch (start us, length us, event | category | flops | bytes accessed | tf_op | source)
XLA Modules:
  0.0 189.9 jit_solution(7021989027191546561)
XLA Ops:
  6.5 1.3 copy.61
  7.9 6.1 %collective-permute-start = (f32[32,1,16,128]{3,2,0,1:T(8,128)S(1)}, f32[32,1,16,128]{3,2,0,1:T(8,128)S(1)}, u32[]{:S(2)}, u32[]{:S(2)}) collective-permute-start(f32[32,1,16,128]{3,2,0,1:T(8,128)S(1)} %get-tuple-element.464), channel_id=1, source_target_pairs={{4,0},{8,4},{12,8},{16,12},{20,16},{24,20},{28,24},{0,28},{5,1},{9... | collective-permute-start | bytes 786440 | tf_op jit(solution)/shard_map/ppermute | solution.py:19
  14.1 3.1 %fusion.87 = (f32[32,4,15,128]{3,2,0,1:T(8,128)}, f32[32,4,15,128]{3,2,0,1:T(8,128)}) fusion(f32[32,4,16,128]{3,2,0,1:T(8,128)} %bitcast.365), kind=kLoop, calls=%fused_computation.139 | loop fusion | bytes 3932160 | tf_op jit(solution)/shard_map/jit(_roll_static)/slice | solution.py:27
  17.2 1.6 fusion.89
  18.9 1.7 fusion.90
  20.6 6.0 %all_gather.12 = f32[3,4,16,128]{3,1,0,2:T(4,128)S(1)} all-gather(f32[3,4,4,128]{3,1,0,2:T(4,128)S(1)} %copy.29), channel_id=1, replica_groups=mesh['space'=8,'field'=4] {'field'}, dimensions={2}, use_global_device_ids=true | all-gather | bytes 122880 | tf_op jit(solution)/shard_map/all_gather | solution.py:101
  29.2 5.2 %all_gather.13 = f32[4,16,128]{2,0,1:T(4,128)S(1)} all-gather(f32[4,4,128]{2,0,1:T(4,128)S(1)} %copy.33), channel_id=1, replica_groups=mesh['space'=8,'field'=4] {'field'}, dimensions={1}, use_global_device_ids=true | all-gather | bytes 40960 | tf_op jit(solution)/shard_map/all_gather | solution.py:102
  34.4 5.2 %all_gather.14 = f32[4,16,128]{2,0,1:T(4,128)S(1)} all-gather(f32[4,4,128]{2,0,1:T(4,128)S(1)} %copy.36), channel_id=1, replica_groups=mesh['space'=8,'field'=4] {'field'}, dimensions={1}, use_global_device_ids=true | all-gather | bytes 40960 | tf_op jit(solution)/shard_map/all_gather | solution.py:103
  39.6 5.2 %all_gather.15 = f32[4,16,128]{2,0,1:T(4,128)S(1)} all-gather(f32[4,4,128]{2,0,1:T(4,128)S(1)} %copy.38), channel_id=1, replica_groups=mesh['space'=8,'field'=4] {'field'}, dimensions={1}, use_global_device_ids=true | all-gather | bytes 40960 | tf_op jit(solution)/shard_map/all_gather | solution.py:104
  46.8 5.6 %all-reduce.3.cloned.1.call-done = f32[32,4,16,128]{3,2,0,1:T(8,128)} async-done(((f32[32,4,16,128]{3,2,0,1:T(8,128)}), f32[32,4,16,128]{3,2,0,1:T(8,128)}) %all-reduce.3.cloned.1.call-update) | async-done | bytes 1048592 | tf_op jit(solution)/shard_map/psum | solution.py:108
  52.5 3.9 %multiply_subtract_fusion.1 = f32[32,4,16,128]{3,2,0,1:T(8,128)S(1)} fusion(f32[32,4,16,128]{3,2,0,1:T(8,128)S(1)} %bitcast.369, f32[32,4,16,128]{3,2,0,1:T(8,128)} %all-reduce.3.cloned.1.call-done, f32[32,4,16,127]{3,2,0,1:T(8,128)} %get-tuple-element.470, f32[32,4,16,1]{3,2,0,1:T(8,128)} %get-tuple-element.472, f32[32,4,16,1]{3,2,0,1:T(8,128)} %get-tuple-element.471, ...), kind=kLoop, calls=%fused_computation.125 | loop fusion | flops 9175040 | bytes 8060940 | tf_op jit(solution)/shard_map/sub | solution.py:39
  56.4 43.6 %while.30 = (s32[]{:T(128)}, f32[32,4,16,128]{3,2,0,1:T(8,128)S(1)}, f32[206]{0:T(256)S(1)}, f32[206,1]{0,1:T(1,128)S(1)}, f32[4,16,128]{2,1,0:T(8,128)S(1)}, /*...) while((s32[]{:T(128)}, ...), condition=%wide.region_2.3_spmd, body=%wide.region_1.2_spmd.sunk | while | flops 427352064 | bytes 22643992 | solution.py:83
  56.9 1.7 fusion.202
  59.1 1.7 fusion.203
  61.2 1.7 fusion.204
  63.4 1.7 fusion.205
  65.5 1.7 fusion.206
  67.8 1.7 fusion.202
  70.0 1.7 fusion.203
  72.1 1.7 fusion.204
  74.3 1.7 fusion.205
  76.4 1.7 fusion.206
  78.7 1.7 fusion.202
  80.9 1.7 fusion.203
  83.0 1.7 fusion.204
  85.2 1.7 fusion.205
  87.3 1.7 fusion.206
  89.6 1.7 fusion.202
  91.8 1.7 fusion.203
  93.9 1.7 fusion.204
  96.1 1.7 fusion.205
  98.2 1.7 fusion.206
  100.1 1.3 fusion.82
  101.4 1.6 fusion.84
  103.8 4.5 %collective-permute-start.2 = (f32[32,1,16,128]{3,2,0,1:T(8,128)}, f32[32,1,16,128]{3,2,0,1:T(8,128)S(1)}, u32[]{:S(2)}, u32[]{:S(2)}) collective-permute-start(f32[32,1,16,128]{3,2,0,1:T(8,128)} %get-tuple-element.454), channel_id=1, source_target_pairs={{4,0},{8,4},{12,8},{16,12},{20,16},{24,20},{28,24},{0,28},{5,1},{9... | collective-permute-start | bytes 786440 | tf_op jit(solution)/shard_map/ppermute | solution.py:19
  108.2 1.7 fusion.85
  110.0 3.3 %collective-permute-done.2 = f32[32,1,16,128]{3,2,0,1:T(8,128)S(1)} collective-permute-done((f32[32,1,16,128]{3,2,0,1:T(8,128)}, f32[32,1,16,128]{3,2,0,1:T(8,128)S(1)}, u32[]{:S(2)}, u32[]{:S(2)}) %collective-permute-start.2) | collective-permute-done | bytes 262176 | tf_op jit(solution)/shard_map/ppermute | solution.py:19
  113.3 4.6 %collective-permute-done.3 = f32[32,1,16,128]{3,2,0,1:T(8,128)S(1)} collective-permute-done((f32[32,1,16,128]{3,2,0,1:T(8,128)S(1)}, f32[32,1,16,128]{3,2,0,1:T(8,128)S(1)}, u32[]{:S(2)}, u32[]{:S(2)}) %collective-permute-start.3) | collective-permute-done | bytes 262176 | tf_op jit(solution)/shard_map/ppermute | solution.py:18
  117.9 22.7 %all-reduce.5.cloned.1.call-done = f32[32,4,16,128]{3,2,0,1:T(8,128)} async-done(((f32[32,4,16,128]{3,2,0,1:T(8,128)}), f32[32,4,16,128]{3,2,0,1:T(8,128)}) %all-reduce.5.cloned.1.call-update) | async-done | bytes 1048592 | tf_op jit(solution)/shard_map/psum | solution.py:108
  140.6 4.4 %multiply_subtract_fusion = f32[32,4,16,128]{3,2,0,1:T(8,128)} fusion(f32[32,4,16,128]{3,2,0,1:T(8,128)S(1)} %copy-done.1, f32[32,4,16,128]{3,2,0,1:T(8,128)} %all-reduce.5.cloned.1.call-done, f32[32,4,16,127]{3,2,0,1:T(8,128)} %get-tuple-element.460, f32[32,4,16,1]{3,2,0,1:T(8,128)} %get-tuple-element.462, f32[32,4,16,1]{3,2,0,1:T(8,128)} %get-tuple-element.461, ...), kind=kLoop, calls=%fused_computation.124 | loop fusion | flops 9175040 | bytes 8060940 | tf_op jit(solution)/shard_map/sub | solution.py:39
  145.0 35.8 %while.31 = (s32[]{:T(128)}, f32[32,4,16,128]{3,2,0,1:T(8,128)}, f32[206]{0:T(256)S(1)}, f32[206,1]{0,1:T(1,128)S(1)}, f32[4,16,128]{2,1,0:T(8,128)S(1)}, /*inde...) while((s32[]{:T(128)}, f32[32,4,16,128]{3,2,0,1:T(8,128)}, ...), condition=%wide.region_5.6_spmd, body=%wide.region_4.5_spmd.sunk | while | flops 427352064 | bytes 22644500 | solution.py:83
  145.0 1.0 constant_dynamic-slice_fusion.5
  146.4 1.0 fusion.230
  147.8 1.0 fusion.231
  149.3 1.0 fusion.232
  150.7 1.0 fusion.233
  152.1 1.0 fusion.234
  153.9 1.0 constant_dynamic-slice_fusion.5
  155.3 1.0 fusion.230
  156.8 1.0 fusion.231
  158.2 1.0 fusion.232
  159.6 1.0 fusion.233
  161.1 1.0 fusion.234
  164.3 1.0 fusion.230
  165.7 1.0 fusion.231
  167.1 1.0 fusion.232
  168.6 1.0 fusion.233
  170.0 1.0 fusion.234
  173.2 1.0 fusion.230
  174.6 1.0 fusion.231
  176.1 1.0 fusion.232
  177.5 1.0 fusion.233
  178.9 1.0 fusion.234
  180.7 2.3 %copy.60 = f32[32,4,16,128]{3,2,1,0:T(8,128)} copy(f32[32,4,16,128]{3,2,0,1:T(8,128)} %get-tuple-element.388) | data formatting | bytes 2097152 | tf_op jit(solution)/shard_map/while | solution.py:83
  (123 shorter events, 24.0 us)
Async XLA Ops:
  6.5 45.9 %all-reduce.3.cloned.1.call-start = ((), (), s32[]{:S(2)}) async-start(), calls=%async_computation | async-start | bytes 2097152 | tf_op jit(solution)/shard_map/psum | solution.py:108
  7.9 6.1 %copy-start.2 = (f32[1,32,4,16,128]{4,3,1,2,0:T(8,128)}, f32[1,32,4,16,128]{4,3,1,2,0:T(8,128)S(1)}, u32[]{:S(2)}) copy-start(f32[1,32,4,16,128]{4,3,1,2,0:T(8,128)S(1)} %copy.61) | copy-start | bytes 3145732
  7.9 38.9 %collective-permute-start = (f32[32,1,16,128]{3,2,0,1:T(8,128)S(1)}, f32[32,1,16,128]{3,2,0,1:T(8,128)S(1)}, u32[]{:S(2)}, u32[]{:S(2)}) collective-permute-start(f32[32,1,16,128]{3,2,0,1:T(8,128)S(1)} %get-tuple-element.464), channel_id=1, source_target_pairs={{4,0},{8,4},{12,8},{16,12},{20,16},{24,20},{28,24},{0,28},{5,1},{9... | collective-permute-start | bytes 786440 | tf_op jit(solution)/shard_map/ppermute | solution.py:19
  14.0 32.9 %collective-permute-start.1 = (f32[32,1,16,128]{3,2,0,1:T(8,128)S(1)}, f32[32,1,16,128]{3,2,0,1:T(8,128)S(1)}, u32[]{:S(2)}, u32[]{:S(2)}) collective-permute-start(f32[32,1,16,128]{3,2,0,1:T(8,128)S(1)} %get-tuple-element.463), channel_id=1, source_target_pairs={{0,4},{4,8},{8,12},{12,16},{16,20},{20,24},{24,28},{28,0},{1,5},{5... | collective-permute-start | bytes 786440 | tf_op jit(solution)/shard_map/ppermute | solution.py:18
  14.0 3.2 %copy-start.3 = (f32[1,32,4,16,128]{4,3,1,2,0:T(8,128)S(1)}, f32[1,32,4,16,128]{4,3,1,2,0:T(8,128)}, u32[]{:S(2)}) copy-start(f32[1,32,4,16,128]{4,3,1,2,0:T(8,128)} %copy-done.2) | copy-start | bytes 3145732
  14.0 126.6 %all-reduce.5.cloned.1.call-start = ((), (), s32[]{:S(2)}) async-start(), calls=%async_computation.1 | async-start | bytes 2097152 | tf_op jit(solution)/shard_map/psum | solution.py:108
  18.8 1.7 copy-start.5
  18.8 7.7 %copy-start.6 = (f32[2,1,3]{2,1,0:T(1,128)S(1)}, f32[2,1,3]{2,1,0:T(1,128)}, u32[]{:S(2)}) copy-start(f32[2,1,3]{2,1,0:T(1,128)} %param.20) | copy-start | bytes 76
  18.8 10.3 %copy-start.7 = (f32[4,4,128]{2,1,0:T(4,128)S(1)}, f32[4,4,128]{2,1,0:T(4,128)}, u32[]{:S(2)}) copy-start(f32[4,4,128]{2,1,0:T(4,128)} %param.17) | copy-start | bytes 24580
  18.8 10.3 %copy-start.8 = (f32[4,4,128]{2,1,0:T(4,128)S(1)}, f32[4,4,128]{2,1,0:T(4,128)}, u32[]{:S(2)}) copy-start(f32[4,4,128]{2,1,0:T(4,128)} %param.18) | copy-start | bytes 24580
  18.8 20.7 %copy-start.9 = (f32[4,4,128]{2,1,0:T(4,128)S(1)}, f32[4,4,128]{2,1,0:T(4,128)}, u32[]{:S(2)}) copy-start(f32[4,4,128]{2,1,0:T(4,128)} %param.19) | copy-start | bytes 24580
  18.9 25.9 %copy-start.10 = (f32[206]{0:T(256)S(1)}, f32[206]{0:T(256)}, u32[]{:S(2)}) copy-start(f32[206]{0:T(256)} %param.25) | copy-start | bytes 2476
  52.5 3.9 %copy-start.4 = (bf16[206,32]{0,1:T(8,128)(2,1)S(1)}, bf16[206,32]{0,1:T(8,128)(2,1)}, u32[]{:S(2)}) copy-start(bf16[206,32]{0,1:T(8,128)(2,1)} %param.21) | copy-start | bytes 39556
  52.5 4.0 %copy-start.11 = (bf16[206,32]{0,1:T(8,128)(2,1)S(1)}, bf16[206,32]{0,1:T(8,128)(2,1)}, u32[]{:S(2)}) copy-start(bf16[206,32]{0,1:T(8,128)(2,1)} %param.22) | copy-start | bytes 39556
  52.5 4.0 %copy-start.13 = (f32[206]{0:T(256)S(1)}, f32[206]{0:T(256)}, u32[]{:S(2)}) copy-start(f32[206]{0:T(256)} %param.24) | copy-start | bytes 2476
  100.1 3.0 %copy-start = (f32[32,4,16,128]{3,2,0,1:T(8,128)}, f32[32,4,16,128]{3,2,0,1:T(8,128)S(1)}, u32[]{:S(2)}) copy-start(f32[32,4,16,128]{3,2,0,1:T(8,128)S(1)} %get-tuple-element.387) | copy-start | bytes 3145732
  103.8 4.5 %copy-start.1 = (f32[32,4,16,128]{3,2,0,1:T(8,128)S(1)}, f32[32,4,16,128]{3,2,0,1:T(8,128)}, u32[]{:S(2)}) copy-start(f32[32,4,16,128]{3,2,0,1:T(8,128)} %copy-done) | copy-start | bytes 3145732
  103.8 9.6 %collective-permute-start.2 = (f32[32,1,16,128]{3,2,0,1:T(8,128)}, f32[32,1,16,128]{3,2,0,1:T(8,128)S(1)}, u32[]{:S(2)}, u32[]{:S(2)}) collective-permute-start(f32[32,1,16,128]{3,2,0,1:T(8,128)} %get-tuple-element.454), channel_id=1, source_target_pairs={{4,0},{8,4},{12,8},{16,12},{20,16},{24,20},{28,24},{0,28},{5,1},{9... | collective-permute-start | bytes 786440 | tf_op jit(solution)/shard_map/ppermute | solution.py:19
  108.2 9.7 %collective-permute-start.3 = (f32[32,1,16,128]{3,2,0,1:T(8,128)S(1)}, f32[32,1,16,128]{3,2,0,1:T(8,128)S(1)}, u32[]{:S(2)}, u32[]{:S(2)}) collective-permute-start(f32[32,1,16,128]{3,2,0,1:T(8,128)S(1)} %get-tuple-element.453), channel_id=1, source_target_pairs={{0,4},{4,8},{8,12},{12,16},{16,20},{20,24},{24,28},{28,0},{1,5},{5... | collective-permute-start | bytes 786440 | tf_op jit(solution)/shard_map/ppermute | solution.py:18
  140.6 4.4 %copy-start.12 = (bf16[32,206]{1,0:T(8,128)(2,1)S(1)}, bf16[32,206]{1,0:T(8,128)(2,1)}, u32[]{:S(2)}) copy-start(bf16[32,206]{1,0:T(8,128)(2,1)} %get-tuple-element.655) | copy-start | bytes 39556
Sparse Core Ops, SparseCore 0:
  14.1 38.2 all-reduce.2
  103.9 36.6 all-reduce.4
where the time goes:
time: 192 us; the launch traced here: 190 us
  matrix products  71.1 us (37%)
  waiting for transfers between devices  36.2 us (19%)
  local copies, waits for them, and re-layouts  23.9 us (12%)
  blocking collectives  21.5 us (11%)
  between operations  17.4 us (9%)
  starting transfers between devices  10.6 us (6%)
  other arithmetic  8.37 us (4%)
    dot_general x40, matrix products, react(): jnp.dot(species_yield_weights, rates, preferred_element_type=jnp.float32)  54.5 us
    psum x2, waiting for transfers between devices, body(): mean = lax.psum(current, 'field') / fields  28.3 us
    dot_general x40, matrix products, react(): jnp.dot(left_bilinear_weights, lowered, preferred_element_type=jnp.float32)  16.6 us
    ppermute x2, starting transfers between devices, extended(): after = lax.ppermute(leading, axis, down)  10.5 us
    sub x2, other arithmetic, transport(): current - advect + spreading_strength * laplace + noise  8.33 us
    slice x4, local copies, waits for them, and re-layouts, transport(): z_plus = jnp.roll(current, -1, 3)  6.63 us
    all_gather x1, blocking collectives, body(): lax.all_gather(filtered_motion, 'field', axis=2, tiled=True)  5.96 us
    all_gather x1, blocking collectives, body(): lax.all_gather(thermal_level, 'field', axis=1, tiled=True)  5.19 us
  transfers between devices with their start and end apart: 6, of which 4 were waited for; matrix products, arithmetic and copies ran while one was open for 5% of the time, Pallas kernels for 0%

commit v1 on v0

--- a/solution.py
+++ b/solution.py
@@ -105,7 +105,7 @@
     )
     current = composition_vector[0]
     for step in range(STEPS):
-        mean = lax.psum(current, "field") / fields
+        mean = jnp.sum(lax.all_gather(current, "field"), axis=0) / fields
         padded = extended(current, (("space", 1),), 1)
         carried_ensemble = transport(
             padded,

time: 192 us -> 187 us (0.974)
  waiting for transfers between devices: 36.2 us -> 25.7 us
  other arithmetic: 8.37 us -> 15 us
  local copies, waits for them, and re-layouts: 23.9 us -> 21.5 us
    psum x2 -> x0, waiting for transfers between devices: 28.3 us -> none  [body(): mean = lax.psum(current, 'field') / fields]
    all_gather x0 -> x2, waiting for transfers between devices: none -> 25 us  [body(): mean = jnp.sum(lax.all_gather(current, 'field'), axis=0) / fields]
    reduce_sum x0 -> x2, other arithmetic: none -> 7.29 us  [body(): mean = jnp.sum(lax.all_gather(current, 'field'), axis=0) / fields]
    ppermute x2, waiting for transfers between devices: 4.59 us -> 0.01 us  [extended(): before = lax.ppermute(last, axis, up)]
    ppermute x2, starting transfers between devices: 0.01 us -> 4.34 us  [extended(): before = lax.ppermute(last, axis, up)]
    ppermute x2, starting transfers between devices: 10.5 us -> 6.39 us  [extended(): after = lax.ppermute(leading, axis, down)]
    ppermute x2, waiting for transfers between devices: 3.33 us -> 0.01 us  [extended(): after = lax.ppermute(leading, axis, down)]
    slice x2, local copies, waits for them, and re-layouts: 0.76 us -> 3.83 us  [extended(): last = lax.slice_in_dim(value, length - width, length, axis=dim)]
  transfers between devices with their start and end apart: 6 -> 6, of which waited for: 4 -> 2; matrix products, arithmetic and copies ran while one was open for 5% -> 11% of each run, Pallas kernels for 0% -> 0%
where the time goes in v1:
time: 187 us; the launch traced here: 185 us
  matrix products  71.1 us (38%)
  waiting for transfers between devices  25.7 us (14%)
  blocking collectives  22.3 us (12%)
  local copies, waits for them, and re-layouts  21.5 us (11%)
  between operations  17.4 us (9%)
  other arithmetic  15 us (8%)
  starting transfers between devices  10.8 us (6%)
    dot_general x40, matrix products, react(): jnp.dot(species_yield_weights, rates, preferred_element_type=jnp.float32)  54.5 us
    all_gather x2, waiting for transfers between devices, body(): mean = jnp.sum(lax.all_gather(current, 'field'), axis=0) / fields  25 us
    dot_general x40, matrix products, react(): jnp.dot(left_bilinear_weights, lowered, preferred_element_type=jnp.float32)  16.6 us
    sub x2, other arithmetic, transport(): current - advect + spreading_strength * laplace + noise  7.69 us
    reduce_sum x2, other arithmetic, body(): mean = jnp.sum(lax.all_gather(current, 'field'), axis=0) / fields  7.29 us
    ppermute x2, starting transfers between devices, extended(): after = lax.ppermute(leading, axis, down)  6.39 us
    all_gather x1, blocking collectives, body(): lax.all_gather(filtered_motion, 'field', axis=2, tiled=True)  6.16 us
    slice x4, local copies, waits for them, and re-layouts, transport(): z_plus = jnp.roll(current, -1, 3)  5.53 us
  transfers between devices with their start and end apart: 6, of which 2 were waited for; matrix products, arithmetic and copies ran while one was open for 11% of the time, Pallas kernels for 0%

profile of v1, /device:TPU:0, one launch (start us, length us, event | category | flops | bytes accessed | tf_op | source)
XLA Modules:
  0.0 184.6 jit_solution(12673181378162679451)
XLA Ops:
  7.3 1.9 %fusion.89 = (f32[32,1,16,128]{3,2,1,0:T(8,128)}, f32[32,1,16,128]{3,2,1,0:T(8,128)}) fusion(f32[32,4,16,128]{3,2,1,0:T(8,128)} %bitcast.365), kind=kLoop, calls=%fused_computation.139 | loop fusion | bytes 1048576 | tf_op jit(solution)/shard_map/slice | solution.py:16
  9.3 3.0 %collective-permute-start.1 = (f32[32,1,16,128]{3,2,1,0:T(8,128)}, f32[32,1,16,128]{3,2,1,0:T(8,128)}, u32[]{:S(2)}, u32[]{:S(2)}) collective-permute-start(f32[32,1,16,128]{3,2,1,0:T(8,128)} %get-tuple-element.479), channel_id=1, source_target_pairs={{0,4},{4,8},{8,12},{12,16},{16,20},{20,24},{24,28},{28,0},{1,5},{5... | collective-permute-start | bytes 786440 | tf_op jit(solution)/shard_map/ppermute | solution.py:18
  12.3 3.0 %collective-permute-start = (f32[32,1,16,128]{3,2,1,0:T(8,128)}, f32[32,1,16,128]{3,2,1,0:T(8,128)}, u32[]{:S(2)}, u32[]{:S(2)}) collective-permute-start(f32[32,1,16,128]{3,2,1,0:T(8,128)} %get-tuple-element.480), channel_id=1, source_target_pairs={{4,0},{8,4},{12,8},{16,12},{20,16},{24,20},{28,24},{0,28},{5,1},{9... | collective-permute-start | bytes 786440 | tf_op jit(solution)/shard_map/ppermute | solution.py:19
  17.9 5.2 %all_gather.22 = f32[4,16,128]{2,0,1:T(4,128)S(1)} all-gather(f32[4,4,128]{2,0,1:T(4,128)S(1)} %copy.79), channel_id=1, replica_groups=mesh['space'=8,'field'=4] {'field'}, dimensions={1}, use_global_device_ids=true | all-gather | bytes 40960 | tf_op jit(solution)/shard_map/all_gather | solution.py:102
  23.1 6.2 %all_gather.21 = f32[3,4,16,128]{3,1,0,2:T(4,128)S(1)} all-gather(f32[3,4,4,128]{3,1,0,2:T(4,128)S(1)} %copy.75), channel_id=1, replica_groups=mesh['space'=8,'field'=4] {'field'}, dimensions={2}, use_global_device_ids=true | all-gather | bytes 122880 | tf_op jit(solution)/shard_map/all_gather | solution.py:101
  29.6 1.8 fusion.93
  31.4 1.7 fusion.92
  33.1 5.5 %all_gather.25 = f32[4,16,128]{2,0,1:T(4,128)S(1)} all-gather(f32[4,4,128]{2,0,1:T(4,128)S(1)} %copy.84), channel_id=1, replica_groups=mesh['space'=8,'field'=4] {'field'}, dimensions={1}, use_global_device_ids=true | all-gather | bytes 40960 | tf_op jit(solution)/shard_map/all_gather | solution.py:104
  38.6 5.5 %all_gather.23 = f32[4,16,128]{2,0,1:T(4,128)S(1)} all-gather(f32[4,4,128]{2,0,1:T(4,128)S(1)} %copy.82), channel_id=1, replica_groups=mesh['space'=8,'field'=4] {'field'}, dimensions={1}, use_global_device_ids=true | all-gather | bytes 40960 | tf_op jit(solution)/shard_map/all_gather | solution.py:103
  44.2 2.9 %all-gather.4.cloned.1.call-done = f32[4,32,4,16,128]{4,3,2,1,0:T(8,128)} async-done(((f32[1,32,4,16,128]{4,3,2,1,0:T(8,128)}), f32[4,32,4,16,128]{4,3,2,1,0:T(8,128)}) %all-gather.4.cloned.1.call-update) | async-done | bytes 4194320 | tf_op jit(solution)/shard_map/all_gather | solution.py:108
  47.1 3.7 %reduce_sum.18 = f32[32,4,16,128]{3,2,1,0:T(8,128)} reduce(f32[4,32,4,16,128]{4,3,2,1,0:T(8,128)} %all-gather.4.cloned.1.call-done, f32[]{:T(128)} %constant.113.clone.1), dimensions={0}, to_apply=%region_0.0 | reduce | flops 786432 | bytes 5242884 | tf_op jit(solution)/shard_map/reduce_sum | solution.py:108
  50.8 3.5 %multiply_subtract_fusion = f32[32,4,16,128]{3,2,1,0:T(8,128)S(1)} fusion(f32[32,4,16,128]{3,2,1,0:T(8,128)S(1)} %bitcast.370, f32[32,4,16,128]{3,2,1,0:T(8,128)} %reduce_sum.18, f32[32,4,16,127]{3,2,1,0:T(8,128)} %get-tuple-element.486, f32[32,4,16,1]{3,2,1,0:T(8,128)} %get-tuple-element.488, f32[32,4,16,1]{3,2,1,0:T(8,128)} %get-tuple-element.487, ...), kind=kLoop, calls=%fused_computation.126 | loop fusion | flops 9175040 | bytes 8060940 | tf_op jit(solution)/shard_map/sub | solution.py:39
  55.0 43.6 %while.30 = (s32[]{:T(128)}, f32[32,4,16,128]{3,2,0,1:T(8,128)S(1)}, f32[206]{0:T(256)S(1)}, f32[206,1]{0,1:T(1,128)S(1)}, f32[4,16,128]{2,1,0:T(8,128)S(1)}, /*...) while((s32[]{:T(128)}, ...), condition=%wide.region_2.3_spmd, body=%wide.region_1.2_spmd.sunk | while | flops 427352064 | bytes 22644000 | solution.py:83
  55.5 1.7 fusion.210
  57.6 1.7 fusion.211
  59.8 1.7 fusion.212
  61.9 1.7 fusion.213
  64.1 1.7 fusion.214
  66.4 1.7 fusion.210
  68.5 1.7 fusion.211
  70.7 1.7 fusion.212
  72.8 1.7 fusion.213
  75.0 1.7 fusion.214
  77.3 1.7 fusion.210
  79.5 1.7 fusion.211
  81.6 1.7 fusion.212
  83.8 1.7 fusion.213
  85.9 1.7 fusion.214
  88.2 1.7 fusion.210
  90.4 1.7 fusion.211
  92.5 1.7 fusion.212
  94.7 1.7 fusion.213
  96.8 1.7 fusion.214
  101.6 1.9 %fusion.84 = (f32[32,1,16,128]{3,2,1,0:T(8,128)}, f32[32,1,16,128]{3,2,1,0:T(8,128)}) fusion(f32[32,4,16,128]{3,2,0,1:T(8,128)} %copy-done), kind=kLoop, calls=%fused_computation.134 | loop fusion | bytes 1048576 | tf_op jit(solution)/shard_map/slice | solution.py:16
  103.5 1.4 collective-permute-start.3
  104.8 3.3 %collective-permute-start.2 = (f32[32,1,16,128]{3,2,1,0:T(8,128)}, f32[32,1,16,128]{3,2,1,0:T(8,128)}, u32[]{:S(2)}, u32[]{:S(2)}) collective-permute-start(f32[32,1,16,128]{3,2,1,0:T(8,128)} %get-tuple-element.470), channel_id=1, source_target_pairs={{4,0},{8,4},{12,8},{16,12},{20,16},{24,20},{28,24},{0,28},{5,1},{9... | collective-permute-start | bytes 786440 | tf_op jit(solution)/shard_map/ppermute | solution.py:19
  108.5 1.7 fusion.85
  110.2 1.7 fusion.87
  112.1 22.0 %all-gather.6.cloned.1.call-done = f32[128,4,16,128]{3,2,0,1:T(8,128)} async-done(((f32[32,4,16,128]{3,2,0,1:T(8,128)}), f32[128,4,16,128]{3,2,0,1:T(8,128)}) %all-gather.6.cloned.1.call-update) | async-done | bytes 4194320 | tf_op jit(solution)/shard_map/all_gather | solution.py:108
  134.2 3.6 %reduce_sum.19 = f32[32,4,16,128]{3,2,0,1:T(8,128)} reduce(f32[4,32,4,16,128]{4,3,1,0,2:T(8,128)} %bitcast.377, f32[]{:T(128)} %constant.113.clone.1), dimensions={0}, to_apply=%region_3.4 | reduce | flops 786432 | bytes 5242884 | tf_op jit(solution)/shard_map/reduce_sum | solution.py:108
  137.8 4.2 %fusion.80 = f32[32,4,16,128]{3,2,1,0:T(8,128)} fusion(f32[32,4,16,128]{3,2,1,0:T(8,128)S(1)} %copy.99, f32[32,4,16,128]{3,2,0,1:T(8,128)} %reduce_sum.19, f32[32,4,16,127]{3,2,1,0:T(8,128)} %get-tuple-element.476, f32[32,4,16,1]{3,2,1,0:T(8,128)S(1)} %get-tuple-element.478, f32[32,4,16,1]{3,2,1,0:T(8,128)S(1)} %get-tuple-element.477, ...), kind=kLoop, calls=%fused_computation.125 | loop fusion | flops 9175040 | bytes 8060940 | tf_op jit(solution)/shard_map/sub | solution.py:39
  142.0 35.8 %while.31 = (s32[]{:T(128)}, f32[32,4,16,128]{3,2,1,0:T(8,128)}, f32[206]{0:T(256)S(1)}, f32[206,1]{0,1:T(1,128)S(1)}, f32[4,16,128]{2,1,0:T(8,128)S(1)}, /*inde...) while((s32[]{:T(128)}, f32[32,4,16,128]{3,2,1,0:T(8,128)}, ...), condition=%wide.region_5.6_spmd, body=%wide.region_4.5_spmd.sunk | while | flops 427352064 | bytes 22696764 | solution.py:83
  143.4 1.0 fusion.238
  144.9 1.0 fusion.239
  146.3 1.0 fusion.240
  147.7 1.0 fusion.241
  149.2 1.0 fusion.242
  150.9 1.0 constant_dynamic-slice_fusion.5
  152.4 1.0 fusion.238
  153.8 1.0 fusion.239
  155.2 1.0 fusion.240
  156.7 1.0 fusion.241
  158.1 1.0 fusion.242
  159.9 1.0 constant_dynamic-slice_fusion.5
  161.3 1.0 fusion.238
  162.8 1.0 fusion.239
  164.2 1.0 fusion.240
  165.6 1.0 fusion.241
  167.1 1.0 fusion.242
  170.3 1.0 fusion.238
  171.7 1.0 fusion.239
  173.1 1.0 fusion.240
  174.6 1.0 fusion.241
  176.0 1.0 fusion.242
  (129 shorter events, 26.3 us)
Async XLA Ops:
  6.5 22.8 %copy-start.2 = (f32[1,32,4,16,128]{4,3,2,1,0:T(8,128)S(1)}, f32[1,32,4,16,128]{4,3,2,1,0:T(8,128)}, u32[]{:S(2)}) copy-start(f32[1,32,4,16,128]{4,3,2,1,0:T(8,128)} %param.15) | copy-start | bytes 3145732
  6.5 8.8 %copy-start.9 = (f32[206]{0:T(256)S(1)}, f32[206]{0:T(256)}, u32[]{:S(2)}) copy-start(f32[206]{0:T(256)} %param.25) | copy-start | bytes 2476
  6.5 8.8 %copy-start.5 = (f32[2,1,3]{2,1,0:T(1,128)S(1)}, f32[2,1,3]{2,1,0:T(1,128)}, u32[]{:S(2)}) copy-start(f32[2,1,3]{2,1,0:T(1,128)} %param.20) | copy-start | bytes 76
  6.5 11.3 %copy-start.6 = (f32[4,4,128]{2,1,0:T(4,128)S(1)}, f32[4,4,128]{2,1,0:T(4,128)}, u32[]{:S(2)}) copy-start(f32[4,4,128]{2,1,0:T(4,128)} %param.17) | copy-start | bytes 24580
  6.5 11.3 %copy-start.7 = (f32[4,4,128]{2,1,0:T(4,128)S(1)}, f32[4,4,128]{2,1,0:T(4,128)}, u32[]{:S(2)}) copy-start(f32[4,4,128]{2,1,0:T(4,128)} %param.18) | copy-start | bytes 24580
  6.5 11.3 %copy-start.8 = (f32[4,4,128]{2,1,0:T(4,128)S(1)}, f32[4,4,128]{2,1,0:T(4,128)}, u32[]{:S(2)}) copy-start(f32[4,4,128]{2,1,0:T(4,128)} %param.19) | copy-start | bytes 24580
  6.6 11.3 %copy-start.4 = (f32[3,4,4,128]{3,2,1,0:T(4,128)S(1)}, f32[3,4,4,128]{3,2,1,0:T(4,128)}, u32[]{:S(2)}) copy-start(f32[3,4,4,128]{3,2,1,0:T(4,128)} %param.16) | copy-start | bytes 73732
  6.6 40.6 %all-gather.4.cloned.1.call-start = ((), (), s32[]{:S(2)}) async-start(), calls=%async_computation | async-start | bytes 5242880 | tf_op jit(solution)/shard_map/all_gather | solution.py:108
  7.3 126.8 %all-gather.6.cloned.1.call-start = ((), (), s32[]{:S(2)}) async-start(), calls=%async_computation.1 | async-start | bytes 5242880 | tf_op jit(solution)/shard_map/all_gather | solution.py:108
  9.3 41.5 %collective-permute-start.1 = (f32[32,1,16,128]{3,2,1,0:T(8,128)}, f32[32,1,16,128]{3,2,1,0:T(8,128)}, u32[]{:S(2)}, u32[]{:S(2)}) collective-permute-start(f32[32,1,16,128]{3,2,1,0:T(8,128)} %get-tuple-element.479), channel_id=1, source_target_pairs={{0,4},{4,8},{8,12},{12,16},{16,20},{20,24},{24,28},{28,0},{1,5},{5... | collective-permute-start | bytes 786440 | tf_op jit(solution)/shard_map/ppermute | solution.py:18
  12.3 38.6 %collective-permute-start = (f32[32,1,16,128]{3,2,1,0:T(8,128)}, f32[32,1,16,128]{3,2,1,0:T(8,128)}, u32[]{:S(2)}, u32[]{:S(2)}) collective-permute-start(f32[32,1,16,128]{3,2,1,0:T(8,128)} %get-tuple-element.480), channel_id=1, source_target_pairs={{4,0},{8,4},{12,8},{16,12},{20,16},{24,20},{28,24},{0,28},{5,1},{9... | collective-permute-start | bytes 786440 | tf_op jit(solution)/shard_map/ppermute | solution.py:19
  54.3 0.7 copy-start.3
  54.3 0.7 copy-start.10
  54.3 0.7 copy-start.12
  98.6 1.0 copy-start
  99.6 8.5 %copy-start.1 = (f32[32,4,16,128]{3,2,0,1:T(8,128)S(1)}, f32[32,4,16,128]{3,2,0,1:T(8,128)}, u32[]{:S(2)}) copy-start(f32[32,4,16,128]{3,2,0,1:T(8,128)} %copy-done) | copy-start | bytes 3145732
  103.5 34.3 %collective-permute-start.3 = (f32[32,1,16,128]{3,2,1,0:T(8,128)}, f32[32,1,16,128]{3,2,1,0:T(8,128)}, u32[]{:S(2)}, u32[]{:S(2)}) collective-permute-start(f32[32,1,16,128]{3,2,1,0:T(8,128)} %get-tuple-element.469), channel_id=1, source_target_pairs={{0,4},{4,8},{8,12},{12,16},{16,20},{20,24},{24,28},{28,0},{1,5},{5... | collective-permute-start | bytes 786440 | tf_op jit(solution)/shard_map/ppermute | solution.py:18
  104.8 32.9 %collective-permute-start.2 = (f32[32,1,16,128]{3,2,1,0:T(8,128)}, f32[32,1,16,128]{3,2,1,0:T(8,128)}, u32[]{:S(2)}, u32[]{:S(2)}) collective-permute-start(f32[32,1,16,128]{3,2,1,0:T(8,128)} %get-tuple-element.470), channel_id=1, source_target_pairs={{4,0},{8,4},{12,8},{16,12},{20,16},{24,20},{28,24},{0,28},{5,1},{9... | collective-permute-start | bytes 786440 | tf_op jit(solution)/shard_map/ppermute | solution.py:19
  142.0 1.4 copy-start.11
  150.9 1.4 copy-start.11
  159.9 1.4 copy-start.11
  168.8 1.4 copy-start.11
Sparse Core Ops, SparseCore 0:
  8.9 38.1 all-gather.3
  99.8 34.3 all-gather.5
